TPU v7x, 512 devices: a whole 4x4x16 slice. The times are simulated.
512 devices in a mesh: space: 64 (over x, z), node: 4 (over y_hi, core), tm: 2 (over y_lo).
Axes of the slice: x: 4, y: 4 (y_hi: 2, y_lo: 2; y = y_hi * 2 + y_lo), z: 16, core: 2. Of those that a mesh axis runs over, the one named last changes fastest.
Arguments:
- start_old: float32 [2, 512, 128, 256], P('tm', 'space'), may hold values from -4 to 4
- nodes_old: float32 [2, 4, 512, 128, 256], P('tm', 'node', 'space'), may hold values from -4 to 4
Outputs:
- nodes_new: float32 [2, 4, 512, 128, 256], P('tm', 'node', 'space')
- end_new: float32 [2, 512, 128, 256], P('tm', 'space')
All inputs are finite; a program needn't handle non-finite values.
Results may differ from a plain program's by a relative error of at most 0.00002.
Values sent between devices are 32-bit elements; how exact they have to be, the bound alone decides.
A program may use at most 64 MiB of HBM per device.

v0:
```python
import jax
import jax.numpy as jnp
from jax import lax
from jax.sharding import PartitionSpec as P

NODES = 4
PASSES = 4
time_step = 0.25
diffusion = 4.0
reaction = 1.0


def padded_2(block, sides, width):
    for axis, dim in sides:
        count = lax.axis_size(axis)
        forward = [(i, i + 1) for i in range(count - 1)]
        forward.append((count - 1, 0))
        backward = [(target, source) for source, target in forward]
        low = lax.ppermute(
            lax.slice_in_dim(block, block.shape[dim] - width, None, axis=dim), axis, forward
        )
        high = lax.ppermute(lax.slice_in_dim(block, 0, width, axis=dim), axis, backward)
        block = jnp.concatenate([low, block, high], axis=dim)
    return block


def shifted_2(array, axis, by):
    size = lax.axis_size(axis)
    pairs = [(i, i + by) for i in range(size) if 0 <= i + by < size]
    return lax.ppermute(array, axis, pairs)


def collocation(count):
    points = [-0.8611363115940526, -0.3399810435848563, 0.3399810435848563, 0.8611363115940526]
    raw_weights = [0.3478548451374538, 0.6521451548625461, 0.6521451548625461, 0.3478548451374538]
    node_times = [(point + 1.0) / 2.0 for point in points]
    quadrature = [[0.0 for column in range(count)] for target in range(count)]
    for source in range(count):
        coeffs = [1.0]
        scaling = 1.0
        for other in range(count):
            if other != source:
                other_time = node_times[other]
                shifted = [0.0] + coeffs
                for power in range(len(coeffs)):
                    shifted[power] = shifted[power] - other_time * coeffs[power]
                coeffs = shifted
                scaling = scaling * (node_times[source] - other_time)
        for target in range(count):
            target_time = node_times[target]
            integral = 0.0
            for power in range(len(coeffs)):
                integral = integral + coeffs[power] * target_time ** (power + 1) / (power + 1)
            quadrature[target][source] = integral / scaling
    return (node_times, quadrature, [weight / 2.0 for weight in raw_weights])


def neighbour_sum(padded):
    inner = padded[1:-1]
    total = padded[2:] + padded[:-2]
    total = total + jnp.roll(inner, -1, 1) + jnp.roll(inner, 1, 1)
    total = total + jnp.roll(inner, -1, 2) + jnp.roll(inner, 1, 2)
    return total


def forcing(values, padded):
    laplace = neighbour_sum(padded) - 6.0 * values
    return (laplace, diffusion * laplace + reaction * (values - values * values * values))


def on_device(start_old, nodes_old):
    node_times, quadrature, weights = collocation(NODES)
    node_index = lax.axis_index("node")
    node_time = jnp.asarray(node_times, jnp.float32)[node_index]
    weight_table = jnp.asarray(weights, jnp.float32)
    node_weight = weight_table[node_index]
    quad_table = jnp.asarray(quadrature, jnp.float32)
    state_old = nodes_old[0, 0]
    start_state = start_old[0]
    padded = padded_2(state_old, (("space", 0),), 1)
    laplace_old, force_old = forcing(state_old, padded)
    quad_row = quad_table[node_index]
    shard_piece = lax.all_gather(force_old[None], "node", axis=0, tiled=True)
    quad_part = jnp.sum(quad_row[:, None, None, None] * shard_piece, axis=0)
    weight_part = jnp.sum(weight_table[:, None, None, None] * shard_piece, axis=0)
    end_old = start_state + time_step * weight_part
    received = shifted_2(end_old, "tm", 1)
    begin_state = jnp.where(lax.axis_index("tm") == 0, start_state, received)
    implicit = time_step * diffusion * node_time
    right_side = begin_state + time_step * quad_part - implicit * laplace_old
    divisor = 1.0 + 6.0 * implicit
    iterate = state_old
    for step_index in range(PASSES):
        widened = padded_2(iterate, (("space", 0),), 1)
        iterate = (right_side + implicit * neighbour_sum(widened)) / divisor
    padded_new = padded_2(iterate, (("space", 0),), 1)
    laplace_new, force_new = forcing(iterate, padded_new)
    weighted_new = lax.psum(node_weight * force_new, "node")
    end_new = begin_state + time_step * weighted_new
    return (iterate[None, None], end_new[None])


def solution(mesh):
    return jax.shard_map(
        on_device,
        mesh=mesh,
        in_specs=(P("tm", "space", None, None), P("tm", "node", "space", None, None)),
        out_specs=(P("tm", "node", "space", None, None), P("tm", "space", None, None)),
        check_vma=False,
    )
```

profile of v0, /device:TPU:1, one launch (start us, length us, event | category | flops | bytes accessed | tf_op | source)
XLA Modules:
  0.0 228.6 jit_solution(15902153033855880192)
XLA Ops:
  7.2 1.1 slice_bitcast_fusion.1
  8.3 14.1 %collective-permute-start = (f32[1,128,256]{2,1,0:T(8,128)S(1)}, f32[1,128,256]{2,1,0:T(8,128)S(1)}, u32[]{:S(2)}, u32[]{:S(2)}) collective-permute-start(f32[1,128,256]{2,1,0:T(8,128)S(1)} %get-tuple-element.48), channel_id=1, source_target_pairs={{8,0},{16,8},{24,16},{32,24},{40,32},{48,40},{56,48},{64,56},{72,6... | collective-permute-start | bytes 393224 | tf_op jit(solution)/shard_map/ppermute | solution.py:22
  22.4 1.9 collective-permute-start.1
  24.4 1.4 fusion.63
  25.8 1.9 fusion.62
  27.7 0.2 fusion.60
  27.9 3.5 %collective-permute-done.1 = f32[1,128,256]{2,1,0:T(8,128)S(1)} collective-permute-done((f32[1,128,256]{2,1,0:T(8,128)S(1)}, f32[1,128,256]{2,1,0:T(8,128)S(1)}, u32[]{:S(2)}, u32[]{:S(2)}) %collective-permute-start.1) | collective-permute-done | bytes 131104 | tf_op jit(solution)/shard_map/ppermute | solution.py:19
  31.5 2.2 fusion
  33.8 0.8 dynamic-slice_bitcast_fusion
  34.5 38.3 %all-gather.3.cloned.1.call-done = f32[32,128,256]{2,1,0:T(8,128)} async-done(((f32[8,128,256]{2,1,0:T(8,128)}), f32[32,128,256]{2,1,0:T(8,128)}) %all-gather.3.cloned.1.call-update) | async-done | bytes 4194320 | tf_op jit(solution)/shard_map/all_gather | solution.py:83
  72.8 4.1 %multiply_reduce_fusion.1 = (f32[8,128,256]{2,1,0:T(8,128)S(1)}, f32[8,128,256]{2,1,0:T(8,128)}) fusion(f32[4,8,128,256]{3,2,1,0:T(8,128)} %bitcast.30, f32[4]{0:T(128)S(1)} %copy-done.3, f32[4]{0:T(128)S(1)} %dynamic-slice_bitcast_fusion), kind=kLoop, calls=%fused_computation.1 | loop fusion | flops 3670016 | bytes 6291488 | tf_op jit(solution)/shard_map/reduce_sum | solution.py:85
  76.9 1.1 bitcast_add_fusion
  78.0 2.3 collective-permute-start.2
  80.3 0.7 dynamic_slice.11
  81.0 0.6 dynamic_slice.10
  82.1 20.7 %collective-permute-done.2 = f32[8,128,256]{2,1,0:T(8,128)S(1)} collective-permute-done((f32[8,128,256]{2,1,0:T(8,128)}, f32[8,128,256]{2,1,0:T(8,128)S(1)}, u32[]{:S(2)}, u32[]{:S(2)}) %collective-permute-start.2) | collective-permute-done | bytes 1048608 | tf_op jit(solution)/shard_map/ppermute | solution.py:30
  102.8 2.5 %add_divide_fusion = (f32[8,128,256]{2,1,0:T(8,128)S(1)}, f32[8,128,256]{2,1,0:T(8,128)S(1)}) fusion(f32[8,128,256]{2,1,0:T(8,128)} %get-tuple-element.7, f32[]{:T(128)S(6)} %add.127, f32[]{:T(128)} %bitcast.6, f32[1,1,8,128,256]{4,3,2,1,0:T(8,128)S(1)} %copy-done, f32[8,128,256]{2,1,0:T(8,128)} %get-tuple-element.3, ...), kind=kLoop, calls=%fused_computation.56 | loop fusion | flops 2621440 | bytes 7340041 | tf_op jit(solution)/shard_map/div | solution.py:95
  105.3 0.2 fusion.55
  105.5 0.2 fusion.58
  105.7 0.4 fusion.56
  106.0 7.8 %collective-permute-start.3 = (f32[1,128,256]{2,1,0:T(8,128)S(1)}, f32[1,128,256]{2,1,0:T(8,128)S(1)}, u32[]{:S(2)}, u32[]{:S(2)}) collective-permute-start(f32[1,128,256]{2,1,0:T(8,128)S(1)} %get-tuple-element.46), channel_id=1, source_target_pairs={{8,0},{16,8},{24,16},{32,24},{40,32},{48,40},{56,48},{64,56},{72,6... | collective-permute-start | bytes 393224 | tf_op jit(solution)/shard_map/ppermute | solution.py:22
  113.9 1.9 collective-permute-start.4
  115.8 7.1 %collective-permute-done.4 = f32[1,128,256]{2,1,0:T(8,128)S(1)} collective-permute-done((f32[1,128,256]{2,1,0:T(8,128)S(1)}, f32[1,128,256]{2,1,0:T(8,128)S(1)}, u32[]{:S(2)}, u32[]{:S(2)}) %collective-permute-start.4) | collective-permute-done | bytes 131104 | tf_op jit(solution)/shard_map/ppermute | solution.py:19
  122.9 1.2 fusion.33
  124.1 0.2 fusion.50
  124.3 0.2 fusion.53
  124.5 0.4 fusion.51
  124.9 1.9 collective-permute-start.5
  126.8 3.4 %collective-permute-start.6 = (f32[1,128,256]{2,1,0:T(8,128)S(1)}, f32[1,128,256]{2,1,0:T(8,128)S(1)}, u32[]{:S(2)}, u32[]{:S(2)}) collective-permute-start(f32[1,128,256]{2,1,0:T(8,128)S(1)} %get-tuple-element.37), channel_id=1, source_target_pairs={{0,8},{8,16},{16,24},{24,32},{32,40},{40,48},{48,56},{56,64},{64,7... | collective-permute-start | bytes 393224 | tf_op jit(solution)/shard_map/ppermute | solution.py:19
  130.2 0.4 collective-permute-done.5
  130.6 5.2 %collective-permute-done.6 = f32[1,128,256]{2,1,0:T(8,128)S(1)} collective-permute-done((f32[1,128,256]{2,1,0:T(8,128)S(1)}, f32[1,128,256]{2,1,0:T(8,128)S(1)}, u32[]{:S(2)}, u32[]{:S(2)}) %collective-permute-start.6) | collective-permute-done | bytes 131104 | tf_op jit(solution)/shard_map/ppermute | solution.py:19
  135.9 1.2 fusion.25
  137.1 0.2 fusion.45
  137.5 0.4 fusion.46
  137.9 1.9 collective-permute-start.7
  139.8 3.4 %collective-permute-start.8 = (f32[1,128,256]{2,1,0:T(8,128)S(1)}, f32[1,128,256]{2,1,0:T(8,128)S(1)}, u32[]{:S(2)}, u32[]{:S(2)}) collective-permute-start(f32[1,128,256]{2,1,0:T(8,128)S(1)} %get-tuple-element.27), channel_id=1, source_target_pairs={{0,8},{8,16},{16,24},{24,32},{32,40},{40,48},{48,56},{56,64},{64,7... | collective-permute-start | bytes 393224 | tf_op jit(solution)/shard_map/ppermute | solution.py:19
  143.2 0.4 collective-permute-done.7
  143.6 5.2 %collective-permute-done.8 = f32[1,128,256]{2,1,0:T(8,128)S(1)} collective-permute-done((f32[1,128,256]{2,1,0:T(8,128)S(1)}, f32[1,128,256]{2,1,0:T(8,128)S(1)}, u32[]{:S(2)}, u32[]{:S(2)}) %collective-permute-start.8) | collective-permute-done | bytes 131104 | tf_op jit(solution)/shard_map/ppermute | solution.py:19
  148.8 1.2 fusion.17
  150.1 0.2 fusion.40
  150.5 0.4 fusion.41
  150.9 1.9 collective-permute-start.9
  152.8 3.4 %collective-permute-start.10 = (f32[1,128,256]{2,1,0:T(8,128)S(1)}, f32[1,128,256]{2,1,0:T(8,128)S(1)}, u32[]{:S(2)}, u32[]{:S(2)}) collective-permute-start(f32[1,128,256]{2,1,0:T(8,128)S(1)} %get-tuple-element.17), channel_id=1, source_target_pairs={{0,8},{8,16},{16,24},{24,32},{32,40},{40,48},{48,56},{56,64},{64,7... | collective-permute-start | bytes 393224 | tf_op jit(solution)/shard_map/ppermute | solution.py:19
  156.2 0.4 collective-permute-done.9
  156.6 5.2 %collective-permute-done.10 = f32[1,128,256]{2,1,0:T(8,128)S(1)} collective-permute-done((f32[1,128,256]{2,1,0:T(8,128)S(1)}, f32[1,128,256]{2,1,0:T(8,128)S(1)}, u32[]{:S(2)}, u32[]{:S(2)}) %collective-permute-start.10) | collective-permute-done | bytes 131104 | tf_op jit(solution)/shard_map/ppermute | solution.py:19
  161.8 2.4 %fusion.2 = f32[8,128,256]{2,1,0:T(8,128)} fusion(f32[8,128,256]{2,1,0:T(8,128)S(1)} %fusion.17, f32[1,128,256]{2,1,0:T(8,128)S(1)} %collective-permute-done.10, f32[1,128,256]{2,1,0:T(8,128)S(1)} %collective-permute-done.9, f32[8,1,256]{2,1,0:T(1,128)S(1)} %get-tuple-element.13, f32[8,127,256]{2,1,0:T(8,128)S(1)} %get-tuple-element.15, ...), kind=kLoop, calls=%fused_computation.6 | loop fusion | flops 4980736 | bytes 6553604 | tf_op jit(solution)/shard_map/mul | solution.py:98
  164.3 55.1 %all-reduce.2.cloned.1.call-done = f32[8,128,256]{2,1,0:T(8,128)} async-done(((f32[8,128,256]{2,1,0:T(8,128)}), f32[8,128,256]{2,1,0:T(8,128)}) %all-reduce.2.cloned.1.call-update) | async-done | bytes 1048592 | tf_op jit(solution)/shard_map/psum | solution.py:98
  219.4 2.4 %add_bitcast_fusion = f32[1,8,128,256]{3,2,1,0:T(8,128)} fusion(f32[8,128,256]{2,1,0:T(8,128)} %all-reduce.2.cloned.1.call-done, f32[8,128,256]{2,1,0:T(8,128)S(1)} %collective-permute-done.2, f32[1,8,128,256]{3,2,1,0:T(8,128)S(1)} %copy-done.2, pred[]{:T(512)S(6)} %eq.3), kind=kLoop, calls=%fused_computation.55 | loop fusion | flops 786432 | bytes 4194305 | tf_op jit(solution)/shard_map/broadcast_in_dim | solution.py:100
  (27 shorter events, 0.7 us)
Async XLA Ops:
  7.2 20.5 %copy-start = (f32[1,1,8,128,256]{4,3,2,1,0:T(8,128)S(1)}, f32[1,1,8,128,256]{4,3,2,1,0:T(8,128)}, u32[]{:S(2)}) copy-start(f32[1,1,8,128,256]{4,3,2,1,0:T(8,128)} %param.6) | copy-start | bytes 3145732
  7.2 65.7 %all-gather.3.cloned.1.call-start = ((), (), s32[]{:S(2)}) async-start(), calls=%async_computation.1 | async-start | bytes 5242880 | tf_op jit(solution)/shard_map/all_gather | solution.py:83
  8.3 19.6 %collective-permute-start = (f32[1,128,256]{2,1,0:T(8,128)S(1)}, f32[1,128,256]{2,1,0:T(8,128)S(1)}, u32[]{:S(2)}, u32[]{:S(2)}) collective-permute-start(f32[1,128,256]{2,1,0:T(8,128)S(1)} %get-tuple-element.48), channel_id=1, source_target_pairs={{8,0},{16,8},{24,16},{32,24},{40,32},{48,40},{56,48},{64,56},{72,6... | collective-permute-start | bytes 393224 | tf_op jit(solution)/shard_map/ppermute | solution.py:22
  22.4 9.0 %collective-permute-start.1 = (f32[1,128,256]{2,1,0:T(8,128)S(1)}, f32[1,128,256]{2,1,0:T(8,128)S(1)}, u32[]{:S(2)}, u32[]{:S(2)}) collective-permute-start(f32[1,128,256]{2,1,0:T(8,128)S(1)} %get-tuple-element.49), channel_id=1, source_target_pairs={{0,8},{8,16},{16,24},{24,32},{32,40},{40,48},{48,56},{56,64},{64,7... | collective-permute-start | bytes 393224 | tf_op jit(solution)/shard_map/ppermute | solution.py:19
  31.5 41.4 %copy-start.3 = (f32[4]{0:T(128)S(1)}, f32[4]{0:T(128)}, u32[]{:S(2)}) copy-start(f32[4]{0:T(128)} %constant.30.clone) | copy-start | bytes 52
  33.7 43.2 %copy-start.2 = (f32[1,8,128,256]{3,2,1,0:T(8,128)S(1)}, f32[1,8,128,256]{3,2,1,0:T(8,128)}, u32[]{:S(2)}) copy-start(f32[1,8,128,256]{3,2,1,0:T(8,128)} %param.5) | copy-start | bytes 3145732
  33.7 185.7 %all-reduce.2.cloned.1.call-start = ((), (), s32[]{:S(2)}) async-start(), calls=%async_computation | async-start | bytes 2097152 | tf_op jit(solution)/shard_map/psum | solution.py:98
  72.8 8.1 %copy-start.4 = (f32[4]{0:T(128)S(1)}, f32[4]{0:T(128)}, u32[]{:S(2)}) copy-start(f32[4]{0:T(128)} %constant.29.clone) | copy-start | bytes 52
  78.0 24.7 %collective-permute-start.2 = (f32[8,128,256]{2,1,0:T(8,128)}, f32[8,128,256]{2,1,0:T(8,128)S(1)}, u32[]{:S(2)}, u32[]{:S(2)}) collective-permute-start(f32[8,128,256]{2,1,0:T(8,128)} %bitcast_add_fusion), channel_id=1, source_target_pairs={{0,1},{2,3},{4,5},{6,7},{8,9},{10,11},{12,13},{14,15},{16,17},{18,... | collective-permute-start | bytes 3145736 | tf_op jit(solution)/shard_map/ppermute | solution.py:30
  106.0 9.8 %collective-permute-start.3 = (f32[1,128,256]{2,1,0:T(8,128)S(1)}, f32[1,128,256]{2,1,0:T(8,128)S(1)}, u32[]{:S(2)}, u32[]{:S(2)}) collective-permute-start(f32[1,128,256]{2,1,0:T(8,128)S(1)} %get-tuple-element.46), channel_id=1, source_target_pairs={{8,0},{16,8},{24,16},{32,24},{40,32},{48,40},{56,48},{64,56},{72,6... | collective-permute-start | bytes 393224 | tf_op jit(solution)/shard_map/ppermute | solution.py:22
  113.9 9.0 %collective-permute-start.4 = (f32[1,128,256]{2,1,0:T(8,128)S(1)}, f32[1,128,256]{2,1,0:T(8,128)S(1)}, u32[]{:S(2)}, u32[]{:S(2)}) collective-permute-start(f32[1,128,256]{2,1,0:T(8,128)S(1)} %get-tuple-element.47), channel_id=1, source_target_pairs={{0,8},{8,16},{16,24},{24,32},{32,40},{40,48},{48,56},{56,64},{64,7... | collective-permute-start | bytes 393224 | tf_op jit(solution)/shard_map/ppermute | solution.py:19
  124.9 5.7 %collective-permute-start.5 = (f32[1,128,256]{2,1,0:T(8,128)S(1)}, f32[1,128,256]{2,1,0:T(8,128)S(1)}, u32[]{:S(2)}, u32[]{:S(2)}) collective-permute-start(f32[1,128,256]{2,1,0:T(8,128)S(1)} %get-tuple-element.36), channel_id=1, source_target_pairs={{8,0},{16,8},{24,16},{32,24},{40,32},{48,40},{56,48},{64,56},{72,6... | collective-permute-start | bytes 393224 | tf_op jit(solution)/shard_map/ppermute | solution.py:22
  126.8 9.0 %collective-permute-start.6 = (f32[1,128,256]{2,1,0:T(8,128)S(1)}, f32[1,128,256]{2,1,0:T(8,128)S(1)}, u32[]{:S(2)}, u32[]{:S(2)}) collective-permute-start(f32[1,128,256]{2,1,0:T(8,128)S(1)} %get-tuple-element.37), channel_id=1, source_target_pairs={{0,8},{8,16},{16,24},{24,32},{32,40},{40,48},{48,56},{56,64},{64,7... | collective-permute-start | bytes 393224 | tf_op jit(solution)/shard_map/ppermute | solution.py:19
  137.9 5.7 %collective-permute-start.7 = (f32[1,128,256]{2,1,0:T(8,128)S(1)}, f32[1,128,256]{2,1,0:T(8,128)S(1)}, u32[]{:S(2)}, u32[]{:S(2)}) collective-permute-start(f32[1,128,256]{2,1,0:T(8,128)S(1)} %get-tuple-element.26), channel_id=1, source_target_pairs={{8,0},{16,8},{24,16},{32,24},{40,32},{48,40},{56,48},{64,56},{72,6... | collective-permute-start | bytes 393224 | tf_op jit(solution)/shard_map/ppermute | solution.py:22
  139.8 9.0 %collective-permute-start.8 = (f32[1,128,256]{2,1,0:T(8,128)S(1)}, f32[1,128,256]{2,1,0:T(8,128)S(1)}, u32[]{:S(2)}, u32[]{:S(2)}) collective-permute-start(f32[1,128,256]{2,1,0:T(8,128)S(1)} %get-tuple-element.27), channel_id=1, source_target_pairs={{0,8},{8,16},{16,24},{24,32},{32,40},{40,48},{48,56},{56,64},{64,7... | collective-permute-start | bytes 393224 | tf_op jit(solution)/shard_map/ppermute | solution.py:19
  150.1 11.8 %copy-start.1 = (f32[8,128,256]{2,1,0:T(8,128)}, f32[8,128,256]{2,1,0:T(8,128)S(1)}, u32[]{:S(2)}) copy-start(f32[8,128,256]{2,1,0:T(8,128)S(1)} %fusion.17) | copy-start | bytes 3145732
  150.9 5.7 %collective-permute-start.9 = (f32[1,128,256]{2,1,0:T(8,128)S(1)}, f32[1,128,256]{2,1,0:T(8,128)S(1)}, u32[]{:S(2)}, u32[]{:S(2)}) collective-permute-start(f32[1,128,256]{2,1,0:T(8,128)S(1)} %get-tuple-element.16), channel_id=1, source_target_pairs={{8,0},{16,8},{24,16},{32,24},{40,32},{48,40},{56,48},{64,56},{72,6... | collective-permute-start | bytes 393224 | tf_op jit(solution)/shard_map/ppermute | solution.py:22
  152.8 9.0 %collective-permute-start.10 = (f32[1,128,256]{2,1,0:T(8,128)S(1)}, f32[1,128,256]{2,1,0:T(8,128)S(1)}, u32[]{:S(2)}, u32[]{:S(2)}) collective-permute-start(f32[1,128,256]{2,1,0:T(8,128)S(1)} %get-tuple-element.17), channel_id=1, source_target_pairs={{0,8},{8,16},{16,24},{24,32},{32,40},{40,48},{48,56},{56,64},{64,7... | collective-permute-start | bytes 393224 | tf_op jit(solution)/shard_map/ppermute | solution.py:19
Sparse Core Ops, SparseCore 0:
  33.8 38.9 all-gather.2
  164.4 54.9 all-reduce.1
where the time goes:
time: 229 us
  waiting for transfers between devices  142 us (62%)
  starting transfers between devices  44 us (19%)
  other arithmetic  18.3 us (8%)
  between operations  14.9 us (7%)
  local copies, waits for them, and re-layouts  9.72 us (4%)
    psum x1, waiting for transfers between devices, on_device(): weighted_new = lax.psum(node_weight * force_new, 'node')  55.1 us
    all_gather x1, waiting for transfers between devices, on_device(): shard_piece = lax.all_gather(force_old[None], 'node', axis=0, tiled=True)  38.3 us
    ppermute x5, starting transfers between devices, padded_2(): lax.ppermute(lax.slice_in_dim(block, 0, width, axis=dim), axis, backward)  27.7 us
    ppermute x5, waiting for transfers between devices, padded_2(): lax.ppermute(lax.slice_in_dim(block, block.shape[dim] - width, None, axis...  26.4 us
    ppermute x1, waiting for transfers between devices, shifted_2(): return lax.ppermute(array, axis, pairs)  20.7 us
    ppermute x5, starting transfers between devices, padded_2(): lax.ppermute(lax.slice_in_dim(block, block.shape[dim] - width, None, axis...  13.9 us
    div x4, other arithmetic, on_device(): iterate = (right_side + implicit * neighbour_sum(widened)) / divisor  6.12 us
    slice x10, local copies, waits for them, and re-layouts, neighbour_sum(): total = total + jnp.roll(inner, -1, 2) + jnp.roll(inner, 1, 2)  5.54 us
  transfers between devices with their start and end apart: 13, of which 11 were waited for; matrix products, arithmetic and copies ran while one was open for 2% of the time, Pallas kernels for 0%

commit v1 on v0

--- a/solution.py
+++ b/solution.py
@@ -80,7 +80,9 @@
     padded = padded_2(state_old, (("space", 0),), 1)
     laplace_old, force_old = forcing(state_old, padded)
     quad_row = quad_table[node_index]
-    shard_piece = lax.all_gather(force_old[None], "node", axis=0, tiled=True)
+    block_2 = force_old[None]
+    sent = jnp.stack([block_2] * lax.axis_size("node"))
+    shard_piece = jnp.concatenate(lax.all_to_all(sent, "node", 0, 0), axis=0)
     quad_part = jnp.sum(quad_row[:, None, None, None] * shard_piece, axis=0)
     weight_part = jnp.sum(weight_table[:, None, None, None] * shard_piece, axis=0)
     end_old = start_state + time_step * weight_part

time: 229 us -> 244 us (1.066)
  waiting for transfers between devices: 142 us -> 150 us
  starting transfers between devices: 44 us -> 47.5 us
  local copies, waits for them, and re-layouts: 9.72 us -> 12.3 us
    all_to_all x0 -> x1, waiting for transfers between devices: none -> 48 us  [on_device(): shard_piece = jnp.concatenate(lax.all_to_all(sent, 'node', 0, 0), axis=0)]
    all_gather x1 -> x0, waiting for transfers between devices: 38.3 us -> none  [on_device(): shard_piece = lax.all_gather(force_old[None], 'node', axis=0, tiled=True)]
    all_to_all x0 -> x1, starting transfers between devices: none -> 7.04 us  [on_device(): shard_piece = jnp.concatenate(lax.all_to_all(sent, 'node', 0, 0), axis=0)]
    ppermute x5, starting transfers between devices: 27.7 us -> 22.2 us  [padded_2(): lax.ppermute(lax.slice_in_dim(block, 0, width, axis=dim), axis, backward)]
    another operation x0 -> x1, local copies, waits for them, and re-layouts: none -> 2.51 us  [on_device(): sent = jnp.stack([block_2] * lax.axis_size('node'))]
  transfers between devices with their start and end apart: 13 -> 13, of which waited for: 11 -> 12; matrix products, arithmetic and copies ran while one was open for 2% -> 2% of each run, Pallas kernels for 0% -> 0%
where the time goes in v1:
time: 244 us; the launch traced here: 243 us
  waiting for transfers between devices  150 us (61%)
  starting transfers between devices  47.5 us (19%)
  other arithmetic  18.5 us (8%)
  between operations  15 us (6%)
  local copies, waits for them, and re-layouts  12.3 us (5%)
    psum x1, waiting for transfers between devices, on_device(): weighted_new = lax.psum(node_weight * force_new, 'node')  55.2 us
    all_to_all x1, waiting for transfers between devices, on_device(): shard_piece = jnp.concatenate(lax.all_to_all(sent, 'node', 0, 0), axis=0)  48 us
    ppermute x5, waiting for transfers between devices, padded_2(): lax.ppermute(lax.slice_in_dim(block, block.shape[dim] - width, None, axis...  24.9 us
    ppermute x5, starting transfers between devices, padded_2(): lax.ppermute(lax.slice_in_dim(block, 0, width, axis=dim), axis, backward)  22.2 us
    ppermute x1, waiting for transfers between devices, shifted_2(): return lax.ppermute(array, axis, pairs)  19.8 us
    ppermute x5, starting transfers between devices, padded_2(): lax.ppermute(lax.slice_in_dim(block, block.shape[dim] - width, None, axis...  15 us
    all_to_all x1, starting transfers between devices, on_device(): shard_piece = jnp.concatenate(lax.all_to_all(sent, 'node', 0, 0), axis=0)  7.04 us
    div x4, other arithmetic, on_device(): iterate = (right_side + implicit * neighbour_sum(widened)) / divisor  6.62 us
  transfers between devices with their start and end apart: 13, of which 12 were waited for; matrix products, arithmetic and copies ran while one was open for 2% of the time, Pallas kernels for 0%

profile of v1, /device:TPU:1, one launch (start us, length us, event | category | flops | bytes accessed | tf_op | source)
XLA Modules:
  0.0 242.8 jit_solution(6196258791063640015)
XLA Ops:
  7.2 1.1 slice_bitcast_fusion.1
  8.3 14.1 %collective-permute-start = (f32[1,128,256]{2,1,0:T(8,128)S(1)}, f32[1,128,256]{2,1,0:T(8,128)S(1)}, u32[]{:S(2)}, u32[]{:S(2)}) collective-permute-start(f32[1,128,256]{2,1,0:T(8,128)S(1)} %get-tuple-element.48), channel_id=1, source_target_pairs={{8,0},{16,8},{24,16},{32,24},{40,32},{48,40},{56,48},{64,56},{72,6... | collective-permute-start | bytes 393224 | tf_op jit(solution)/shard_map/ppermute | solution.py:22
  22.4 1.9 collective-permute-start.1
  24.3 1.4 fusion.65
  25.7 1.9 fusion.64
  27.9 3.5 %collective-permute-done.1 = f32[1,128,256]{2,1,0:T(8,128)S(1)} collective-permute-done((f32[1,128,256]{2,1,0:T(8,128)S(1)}, f32[1,128,256]{2,1,0:T(8,128)S(1)}, u32[]{:S(2)}, u32[]{:S(2)}) %collective-permute-start.1) | collective-permute-done | bytes 131104 | tf_op jit(solution)/shard_map/ppermute | solution.py:19
  31.4 1.9 fusion.2
  33.3 2.5 %stack.3 = f32[4,1,8,128,256]{4,3,2,1,0:T(8,128)} broadcast(f32[8,128,256]{2,1,0:T(8,128)S(1)} %get-tuple-element.6), dimensions={2,3,4} | broadcast | bytes 5242880 | tf_op jit(solution)/shard_map/stack | solution.py:84
  35.8 7.0 %all-to-all-start = ((f32[4,1,8,128,256]{4,3,2,1,0:T(8,128)}), f32[4,1,8,128,256]{4,3,2,1,0:T(8,128)}, u32[]{:S(2)}, u32[]{:S(2)}) async-start(f32[4,1,8,128,256]{4,3,2,1,0:T(8,128)} %stack.3), calls=%async_computation | async-start | bytes 8388608 | tf_op jit(solution)/shard_map/all_to_all | solution.py:85
  42.8 0.8 dynamic-slice_bitcast_fusion
  43.6 48.0 %all-to-all-done = f32[4,1,8,128,256]{4,3,2,1,0:T(8,128)} async-done(((f32[4,1,8,128,256]{4,3,2,1,0:T(8,128)}), f32[4,1,8,128,256]{4,3,2,1,0:T(8,128)}, u32[]{:S(2)}, u32[]{:S(2)}) %all-to-all-start) | async-done | bytes 4194336 | tf_op jit(solution)/shard_map/all_to_all | solution.py:85
  91.6 4.1 %fusion = (f32[8,128,256]{2,1,0:T(8,128)S(1)}, f32[8,128,256]{2,1,0:T(8,128)}) fusion(f32[4,1,8,128,256]{4,3,2,1,0:T(8,128)} %all-to-all-done, f32[4]{0:T(128)S(1)} %copy-done.3, f32[4]{0:T(128)S(1)} %dynamic-slice_bitcast_fusion), kind=kLoop, calls=%fused_computation.2 | loop fusion | flops 3670016 | bytes 6291488 | tf_op jit(solution)/shard_map/reduce_sum | solution.py:87
  95.7 1.1 bitcast_add_fusion
  96.8 3.3 %collective-permute-start.2 = (f32[8,128,256]{2,1,0:T(8,128)}, f32[8,128,256]{2,1,0:T(8,128)S(1)}, u32[]{:S(2)}, u32[]{:S(2)}) collective-permute-start(f32[8,128,256]{2,1,0:T(8,128)} %bitcast_add_fusion), channel_id=1, source_target_pairs={{0,1},{2,3},{4,5},{6,7},{8,9},{10,11},{12,13},{14,15},{16,17},{18,... | collective-permute-start | bytes 3145736 | tf_op jit(solution)/shard_map/ppermute | solution.py:30
  100.1 0.7 dynamic_slice.11
  100.7 0.6 dynamic_slice.10
  102.1 19.8 %collective-permute-done.2 = f32[8,128,256]{2,1,0:T(8,128)S(1)} collective-permute-done((f32[8,128,256]{2,1,0:T(8,128)}, f32[8,128,256]{2,1,0:T(8,128)S(1)}, u32[]{:S(2)}, u32[]{:S(2)}) %collective-permute-start.2) | collective-permute-done | bytes 1048608 | tf_op jit(solution)/shard_map/ppermute | solution.py:30
  121.8 2.6 %add_divide_fusion = (f32[8,128,256]{2,1,0:T(8,128)S(1)}, f32[8,128,256]{2,1,0:T(8,128)S(1)}) fusion(f32[8,128,256]{2,1,0:T(8,128)} %get-tuple-element.7, f32[]{:T(128)S(6)} %add.127, f32[]{:T(128)} %bitcast.6, f32[1,1,8,128,256]{4,3,2,1,0:T(8,128)S(1)} %copy-done, f32[8,128,256]{2,1,0:T(8,128)} %get-tuple-element.3, ...), kind=kLoop, calls=%fused_computation.58 | loop fusion | flops 2621440 | bytes 7340041 | tf_op jit(solution)/shard_map/div | solution.py:97
  124.5 0.2 fusion.57
  124.9 0.4 fusion.58
  125.2 2.3 collective-permute-start.3
  127.5 3.0 %collective-permute-start.4 = (f32[1,128,256]{2,1,0:T(8,128)S(1)}, f32[1,128,256]{2,1,0:T(8,128)S(1)}, u32[]{:S(2)}, u32[]{:S(2)}) collective-permute-start(f32[1,128,256]{2,1,0:T(8,128)S(1)} %get-tuple-element.47), channel_id=1, source_target_pairs={{0,8},{8,16},{16,24},{24,32},{32,40},{40,48},{48,56},{56,64},{64,7... | collective-permute-start | bytes 393224 | tf_op jit(solution)/shard_map/ppermute | solution.py:19
  130.5 0.4 collective-permute-done.3
  130.9 5.6 %collective-permute-done.4 = f32[1,128,256]{2,1,0:T(8,128)S(1)} collective-permute-done((f32[1,128,256]{2,1,0:T(8,128)S(1)}, f32[1,128,256]{2,1,0:T(8,128)S(1)}, u32[]{:S(2)}, u32[]{:S(2)}) %collective-permute-start.4) | collective-permute-done | bytes 131104 | tf_op jit(solution)/shard_map/ppermute | solution.py:19
  136.5 1.3 fusion.35
  137.9 0.2 fusion.52
  138.3 0.4 fusion.53
  138.7 1.9 collective-permute-start.5
  140.6 3.4 %collective-permute-start.6 = (f32[1,128,256]{2,1,0:T(8,128)S(1)}, f32[1,128,256]{2,1,0:T(8,128)S(1)}, u32[]{:S(2)}, u32[]{:S(2)}) collective-permute-start(f32[1,128,256]{2,1,0:T(8,128)S(1)} %get-tuple-element.37), channel_id=1, source_target_pairs={{0,8},{8,16},{16,24},{24,32},{32,40},{40,48},{48,56},{56,64},{64,7... | collective-permute-start | bytes 393224 | tf_op jit(solution)/shard_map/ppermute | solution.py:19
  144.0 0.4 collective-permute-done.5
  144.4 5.2 %collective-permute-done.6 = f32[1,128,256]{2,1,0:T(8,128)S(1)} collective-permute-done((f32[1,128,256]{2,1,0:T(8,128)S(1)}, f32[1,128,256]{2,1,0:T(8,128)S(1)}, u32[]{:S(2)}, u32[]{:S(2)}) %collective-permute-start.6) | collective-permute-done | bytes 131104 | tf_op jit(solution)/shard_map/ppermute | solution.py:19
  149.6 1.3 fusion.27
  151.0 0.2 fusion.47
  151.4 0.4 fusion.48
  151.8 1.9 collective-permute-start.7
  153.7 3.4 %collective-permute-start.8 = (f32[1,128,256]{2,1,0:T(8,128)S(1)}, f32[1,128,256]{2,1,0:T(8,128)S(1)}, u32[]{:S(2)}, u32[]{:S(2)}) collective-permute-start(f32[1,128,256]{2,1,0:T(8,128)S(1)} %get-tuple-element.27), channel_id=1, source_target_pairs={{0,8},{8,16},{16,24},{24,32},{32,40},{40,48},{48,56},{56,64},{64,7... | collective-permute-start | bytes 393224 | tf_op jit(solution)/shard_map/ppermute | solution.py:19
  157.1 0.4 collective-permute-done.7
  157.5 5.2 %collective-permute-done.8 = f32[1,128,256]{2,1,0:T(8,128)S(1)} collective-permute-done((f32[1,128,256]{2,1,0:T(8,128)S(1)}, f32[1,128,256]{2,1,0:T(8,128)S(1)}, u32[]{:S(2)}, u32[]{:S(2)}) %collective-permute-start.8) | collective-permute-done | bytes 131104 | tf_op jit(solution)/shard_map/ppermute | solution.py:19
  162.7 1.3 fusion.19
  164.1 0.2 fusion.42
  164.5 0.4 fusion.43
  164.9 1.9 collective-permute-start.9
  166.8 3.4 %collective-permute-start.10 = (f32[1,128,256]{2,1,0:T(8,128)S(1)}, f32[1,128,256]{2,1,0:T(8,128)S(1)}, u32[]{:S(2)}, u32[]{:S(2)}) collective-permute-start(f32[1,128,256]{2,1,0:T(8,128)S(1)} %get-tuple-element.17), channel_id=1, source_target_pairs={{0,8},{8,16},{16,24},{24,32},{32,40},{40,48},{48,56},{56,64},{64,7... | collective-permute-start | bytes 393224 | tf_op jit(solution)/shard_map/ppermute | solution.py:19
  170.2 0.4 collective-permute-done.9
  170.6 5.2 %collective-permute-done.10 = f32[1,128,256]{2,1,0:T(8,128)S(1)} collective-permute-done((f32[1,128,256]{2,1,0:T(8,128)S(1)}, f32[1,128,256]{2,1,0:T(8,128)S(1)}, u32[]{:S(2)}, u32[]{:S(2)}) %collective-permute-start.10) | collective-permute-done | bytes 131104 | tf_op jit(solution)/shard_map/ppermute | solution.py:19
  175.9 2.4 fusion.4
  178.3 55.2 %all-reduce.2.cloned.1.call-done = f32[8,128,256]{2,1,0:T(8,128)} async-done(((f32[8,128,256]{2,1,0:T(8,128)}), f32[8,128,256]{2,1,0:T(8,128)}) %all-reduce.2.cloned.1.call-update) | async-done | bytes 1048592 | tf_op jit(solution)/shard_map/psum | solution.py:100
  233.6 2.4 add_bitcast_fusion
  (27 shorter events, 1.2 us)
Async XLA Ops:
  7.2 20.5 %copy-start = (f32[1,1,8,128,256]{4,3,2,1,0:T(8,128)S(1)}, f32[1,1,8,128,256]{4,3,2,1,0:T(8,128)}, u32[]{:S(2)}) copy-start(f32[1,1,8,128,256]{4,3,2,1,0:T(8,128)} %param.6) | copy-start | bytes 3145732
  8.3 19.6 %collective-permute-start = (f32[1,128,256]{2,1,0:T(8,128)S(1)}, f32[1,128,256]{2,1,0:T(8,128)S(1)}, u32[]{:S(2)}, u32[]{:S(2)}) collective-permute-start(f32[1,128,256]{2,1,0:T(8,128)S(1)} %get-tuple-element.48), channel_id=1, source_target_pairs={{8,0},{16,8},{24,16},{32,24},{40,32},{48,40},{56,48},{64,56},{72,6... | collective-permute-start | bytes 393224 | tf_op jit(solution)/shard_map/ppermute | solution.py:22
  22.4 9.0 %collective-permute-start.1 = (f32[1,128,256]{2,1,0:T(8,128)S(1)}, f32[1,128,256]{2,1,0:T(8,128)S(1)}, u32[]{:S(2)}, u32[]{:S(2)}) collective-permute-start(f32[1,128,256]{2,1,0:T(8,128)S(1)} %get-tuple-element.49), channel_id=1, source_target_pairs={{0,8},{8,16},{16,24},{24,32},{32,40},{40,48},{48,56},{56,64},{64,7... | collective-permute-start | bytes 393224 | tf_op jit(solution)/shard_map/ppermute | solution.py:19
  35.8 55.8 %copy-start.3 = (f32[4]{0:T(128)S(1)}, f32[4]{0:T(128)}, u32[]{:S(2)}) copy-start(f32[4]{0:T(128)} %constant.30.clone) | copy-start | bytes 52
  35.8 55.8 %all-to-all-start = ((f32[4,1,8,128,256]{4,3,2,1,0:T(8,128)}), f32[4,1,8,128,256]{4,3,2,1,0:T(8,128)}, u32[]{:S(2)}, u32[]{:S(2)}) async-start(f32[4,1,8,128,256]{4,3,2,1,0:T(8,128)} %stack.3), calls=%async_computation | async-start | bytes 8388608 | tf_op jit(solution)/shard_map/all_to_all | solution.py:85
  42.8 52.8 %copy-start.2 = (f32[1,8,128,256]{3,2,1,0:T(8,128)S(1)}, f32[1,8,128,256]{3,2,1,0:T(8,128)}, u32[]{:S(2)}) copy-start(f32[1,8,128,256]{3,2,1,0:T(8,128)} %param.5) | copy-start | bytes 3145732
  42.8 190.7 %all-reduce.2.cloned.1.call-start = ((), (), s32[]{:S(2)}) async-start(), calls=%async_computation.1 | async-start | bytes 2097152 | tf_op jit(solution)/shard_map/psum | solution.py:100
  43.6 57.1 %copy-start.4 = (f32[4]{0:T(128)S(1)}, f32[4]{0:T(128)}, u32[]{:S(2)}) copy-start(f32[4]{0:T(128)} %constant.29.clone) | copy-start | bytes 52
  96.8 25.0 %collective-permute-start.2 = (f32[8,128,256]{2,1,0:T(8,128)}, f32[8,128,256]{2,1,0:T(8,128)S(1)}, u32[]{:S(2)}, u32[]{:S(2)}) collective-permute-start(f32[8,128,256]{2,1,0:T(8,128)} %bitcast_add_fusion), channel_id=1, source_target_pairs={{0,1},{2,3},{4,5},{6,7},{8,9},{10,11},{12,13},{14,15},{16,17},{18,... | collective-permute-start | bytes 3145736 | tf_op jit(solution)/shard_map/ppermute | solution.py:30
  125.2 5.7 %collective-permute-start.3 = (f32[1,128,256]{2,1,0:T(8,128)S(1)}, f32[1,128,256]{2,1,0:T(8,128)S(1)}, u32[]{:S(2)}, u32[]{:S(2)}) collective-permute-start(f32[1,128,256]{2,1,0:T(8,128)S(1)} %get-tuple-element.46), channel_id=1, source_target_pairs={{8,0},{16,8},{24,16},{32,24},{40,32},{48,40},{56,48},{64,56},{72,6... | collective-permute-start | bytes 393224 | tf_op jit(solution)/shard_map/ppermute | solution.py:22
  127.5 9.0 %collective-permute-start.4 = (f32[1,128,256]{2,1,0:T(8,128)S(1)}, f32[1,128,256]{2,1,0:T(8,128)S(1)}, u32[]{:S(2)}, u32[]{:S(2)}) collective-permute-start(f32[1,128,256]{2,1,0:T(8,128)S(1)} %get-tuple-element.47), channel_id=1, source_target_pairs={{0,8},{8,16},{16,24},{24,32},{32,40},{40,48},{48,56},{56,64},{64,7... | collective-permute-start | bytes 393224 | tf_op jit(solution)/shard_map/ppermute | solution.py:19
  138.7 5.7 %collective-permute-start.5 = (f32[1,128,256]{2,1,0:T(8,128)S(1)}, f32[1,128,256]{2,1,0:T(8,128)S(1)}, u32[]{:S(2)}, u32[]{:S(2)}) collective-permute-start(f32[1,128,256]{2,1,0:T(8,128)S(1)} %get-tuple-element.36), channel_id=1, source_target_pairs={{8,0},{16,8},{24,16},{32,24},{40,32},{48,40},{56,48},{64,56},{72,6... | collective-permute-start | bytes 393224 | tf_op jit(solution)/shard_map/ppermute | solution.py:22
  140.6 9.0 %collective-permute-start.6 = (f32[1,128,256]{2,1,0:T(8,128)S(1)}, f32[1,128,256]{2,1,0:T(8,128)S(1)}, u32[]{:S(2)}, u32[]{:S(2)}) collective-permute-start(f32[1,128,256]{2,1,0:T(8,128)S(1)} %get-tuple-element.37), channel_id=1, source_target_pairs={{0,8},{8,16},{16,24},{24,32},{32,40},{40,48},{48,56},{56,64},{64,7... | collective-permute-start | bytes 393224 | tf_op jit(solution)/shard_map/ppermute | solution.py:19
  151.8 5.7 %collective-permute-start.7 = (f32[1,128,256]{2,1,0:T(8,128)S(1)}, f32[1,128,256]{2,1,0:T(8,128)S(1)}, u32[]{:S(2)}, u32[]{:S(2)}) collective-permute-start(f32[1,128,256]{2,1,0:T(8,128)S(1)} %get-tuple-element.26), channel_id=1, source_target_pairs={{8,0},{16,8},{24,16},{32,24},{40,32},{48,40},{56,48},{64,56},{72,6... | collective-permute-start | bytes 393224 | tf_op jit(solution)/shard_map/ppermute | solution.py:22
  153.7 9.0 %collective-permute-start.8 = (f32[1,128,256]{2,1,0:T(8,128)S(1)}, f32[1,128,256]{2,1,0:T(8,128)S(1)}, u32[]{:S(2)}, u32[]{:S(2)}) collective-permute-start(f32[1,128,256]{2,1,0:T(8,128)S(1)} %get-tuple-element.27), channel_id=1, source_target_pairs={{0,8},{8,16},{16,24},{24,32},{32,40},{40,48},{48,56},{56,64},{64,7... | collective-permute-start | bytes 393224 | tf_op jit(solution)/shard_map/ppermute | solution.py:19
  164.1 11.8 %copy-start.1 = (f32[8,128,256]{2,1,0:T(8,128)}, f32[8,128,256]{2,1,0:T(8,128)S(1)}, u32[]{:S(2)}) copy-start(f32[8,128,256]{2,1,0:T(8,128)S(1)} %fusion.19) | copy-start | bytes 3145732
  164.9 5.7 %collective-permute-start.9 = (f32[1,128,256]{2,1,0:T(8,128)S(1)}, f32[1,128,256]{2,1,0:T(8,128)S(1)}, u32[]{:S(2)}, u32[]{:S(2)}) collective-permute-start(f32[1,128,256]{2,1,0:T(8,128)S(1)} %get-tuple-element.16), channel_id=1, source_target_pairs={{8,0},{16,8},{24,16},{32,24},{40,32},{48,40},{56,48},{64,56},{72,6... | collective-permute-start | bytes 393224 | tf_op jit(solution)/shard_map/ppermute | solution.py:22
  166.8 9.0 %collective-permute-start.10 = (f32[1,128,256]{2,1,0:T(8,128)S(1)}, f32[1,128,256]{2,1,0:T(8,128)S(1)}, u32[]{:S(2)}, u32[]{:S(2)}) collective-permute-start(f32[1,128,256]{2,1,0:T(8,128)S(1)} %get-tuple-element.17), channel_id=1, source_target_pairs={{0,8},{8,16},{16,24},{24,32},{32,40},{40,48},{48,56},{56,64},{64,7... | collective-permute-start | bytes 393224 | tf_op jit(solution)/shard_map/ppermute | solution.py:19
Sparse Core Ops, SparseCore 0:
  178.4 55.0 all-reduce.1
